TPU v7x, 32 devices: a whole 2x2x4 slice. The times are simulated.
32 devices in a mesh: band: 8 (over z, y), grid: 4 (over x, core).
Axes of the slice: x: 2, y: 2, z: 4, core: 2. Of those that a mesh axis runs over, the one named last changes fastest.
Arguments:
- orbitals: bfloat16 [16, 128, 128, 128], P('band', 'grid'), may hold values from -6 to 6
- occupation: float32 [16], replicated, may hold values from 0.25 to 2
- partner: int32 [8], replicated, may hold values from 0 to 7, as said below
- col_index: int32 [8192], replicated, may hold values from 0 to 16383, as said below
- kernel: float32 [128, 8192], P(None, 'grid'), may hold values from 0.1 to 4
Outputs:
- exchange: float32 [16, 128, 128, 128], P('band', 'grid')
Inputs may be any that keep to these rules, and one draw needn't show every extreme that they name: partner[partner[a]] = a and partner[a] != a for every block a. `col_index`: all entries are distinct; the entries at positions g * 2048 to (g + 1) * 2048 - 1 are columns of the g-th block of 4096 consecutive columns, among them that block's first and last column.
All inputs are finite; a program needn't handle non-finite values.
Results may differ from a plain program's by a relative error of at most 0.0065.
Values may be sent and summed in bfloat16 or wider, within the bound.
No kernel may reach another device: no remote copies, remote signals or barrier semaphores. Data moves between devices by JAX's collectives and lax.ppermute only.
A program may use at most 64 MiB of HBM per device.

v0:
```python
import math
import jax
import jax.numpy as jnp
import numpy as np
from jax import lax
from jax.sharding import PartitionSpec as P

NX = 128
NY = 128
NZ = 128


def tables(length):
    counter = jnp.arange(length, dtype=jnp.int32)
    product = counter[:, None] * counter[None, :] % length
    angles = product.astype(jnp.float32) * (2.0 * math.pi / length)
    return (jnp.cos(angles).astype(jnp.bfloat16), jnp.sin(angles).astype(jnp.bfloat16))


def contract(pattern, left_side, right_side):
    return jnp.einsum(pattern, left_side, right_side, preferred_element_type=jnp.float32)


def fetch_block(block_data, partner):
    band_count = lax.axis_size("band")
    spread = lax.all_to_all(block_data, "band", split_axis=2, concat_axis=2, tiled=True)
    dims = spread.shape
    pieces = spread.reshape(dims[0], dims[1], band_count, dims[2] // band_count, dims[3])
    pieces = jnp.take(pieces, partner, axis=2).reshape(dims)
    return lax.all_to_all(pieces, "band", split_axis=2, concat_axis=2, tiled=True)


def return_block(block_data, partner):
    band_count = lax.axis_size("band")
    spread = lax.all_to_all(
        block_data.astype(jnp.bfloat16), "band", split_axis=2, concat_axis=2, tiled=True
    ).astype(block_data.dtype)
    dims = spread.shape
    pieces = spread.reshape(dims[0], dims[1], band_count, dims[2] // band_count, dims[3])
    pieces = jnp.take(pieces, partner, axis=2).reshape(dims)
    return lax.all_to_all(
        pieces.astype(jnp.bfloat16), "band", split_axis=2, concat_axis=2, tiled=True
    ).astype(pieces.dtype)


def local(orbitals, occupation, partner, col_index, kernel):
    block_bands = orbitals.shape[0]
    slab_rows = orbitals.shape[1]
    half_block = block_bands // 2
    pair_count = block_bands * half_block
    band_pos = lax.axis_index("band")
    partner_block = partner[band_pos]
    theirs = fetch_block(orbitals, partner)
    parity = (band_pos > partner_block).astype(jnp.int32)
    slot_table = np.arange(pair_count)
    left_table = slot_table // half_block
    left_index = jnp.asarray(left_table, jnp.int32)
    right_index = (left_index + parity) % 2 + 2 * jnp.asarray(slot_table % half_block, jnp.int32)
    left_bands = orbitals[left_table]
    right_bands = jnp.take(theirs, right_index, axis=0)
    density = (left_bands.astype(jnp.float32) * right_bands.astype(jnp.float32)).astype(
        jnp.bfloat16
    )
    xcosine, xsines = tables(NX)
    ycosine, ysines = tables(NY)
    zcosine, zsines = tables(NZ)
    ztable = jnp.concatenate([zcosine, -zsines], axis=1)
    first_both = contract("pxyz,zk->pxyk", density, ztable).astype(jnp.bfloat16)
    first_real = first_both[..., :NZ]
    first_imag = first_both[..., NZ:]
    second_real = (
        contract("pxyk,yq->pxqk", first_real, ycosine)
        + contract("pxyk,yq->pxqk", first_imag, ysines)
    ).astype(jnp.bfloat16)
    second_imag = (
        contract("pxyk,yq->pxqk", first_imag, ycosine)
        - contract("pxyk,yq->pxqk", first_real, ysines)
    ).astype(jnp.bfloat16)
    second_real = second_real.reshape(pair_count, slab_rows, NY * NZ)
    second_imag = second_imag.reshape(pair_count, slab_rows, NY * NZ)
    norm_scale = 1.0 / (NX * NY * NZ)
    grid_pos = lax.axis_index("grid")
    column_count = kernel.shape[1]
    column_span = NY * NZ // lax.axis_size("grid")
    local_cols = (
        lax.dynamic_slice_in_dim(col_index, grid_pos * column_count, column_count, 0)
        - grid_pos * column_span
    )
    kern_local = (
        jnp.zeros((NX, column_span), jnp.float32).at[:, local_cols].set(kernel * norm_scale)
    )
    column_real = lax.all_to_all(second_real, "grid", split_axis=2, concat_axis=1, tiled=True)
    column_imag = lax.all_to_all(second_imag, "grid", split_axis=2, concat_axis=1, tiled=True)
    scaled_real = contract("pxc,xk->pkc", column_real, xcosine) + contract(
        "pxc,xk->pkc", column_imag, xsines
    )
    scaled_imag = contract("pxc,xk->pkc", column_imag, xcosine) - contract(
        "pxc,xk->pkc", column_real, xsines
    )
    scaled_real = (scaled_real * kern_local).astype(jnp.bfloat16)
    scaled_imag = (scaled_imag * kern_local).astype(jnp.bfloat16)
    third_real = (
        contract("pkc,xk->pxc", scaled_real, xcosine) - contract("pkc,xk->pxc", scaled_imag, xsines)
    ).astype(jnp.bfloat16)
    third_imag = (
        contract("pkc,xk->pxc", scaled_imag, xcosine) + contract("pkc,xk->pxc", scaled_real, xsines)
    ).astype(jnp.bfloat16)
    back_real = lax.all_to_all(third_real, "grid", split_axis=1, concat_axis=2, tiled=True)
    back_imag = lax.all_to_all(third_imag, "grid", split_axis=1, concat_axis=2, tiled=True)
    back_real = back_real.reshape(pair_count, slab_rows, NY, NZ)
    back_imag = back_imag.reshape(pair_count, slab_rows, NY, NZ)
    fourth_real = (
        contract("pxqk,yq->pxyk", back_real, ycosine) - contract("pxqk,yq->pxyk", back_imag, ysines)
    ).astype(jnp.bfloat16)
    fourth_imag = (
        contract("pxqk,yq->pxyk", back_imag, ycosine) + contract("pxqk,yq->pxyk", back_real, ysines)
    ).astype(jnp.bfloat16)
    fourth_both = jnp.concatenate([fourth_real, fourth_imag], axis=3)
    potential = contract("pxyk,zk->pxyz", fourth_both, ztable)
    own_occ = lax.dynamic_slice_in_dim(occupation, band_pos * block_bands, block_bands, 0)
    their_occ = lax.dynamic_slice_in_dim(occupation, partner_block * block_bands, block_bands, 0)
    right_weight = jnp.take(their_occ, right_index)
    left_weight = jnp.take(own_occ, left_index)
    own_terms = potential * right_weight[:, None, None, None] * right_bands.astype(jnp.float32)
    their_terms = potential * left_weight[:, None, None, None] * left_bands.astype(jnp.float32)
    own_sum = jnp.sum(own_terms.reshape((block_bands, half_block) + own_terms.shape[1:]), axis=1)
    their_sum = jnp.stack(
        [
            jnp.sum(
                jnp.where((right_index == band_number)[:, None, None, None], their_terms, 0.0),
                axis=0,
            )
            for band_number in range(block_bands)
        ]
    )
    returned = return_block(their_sum, partner)
    return -(own_sum + returned)


def solution(mesh):
    in_specs = (P("band", "grid", None, None), P(), P(), P(), P(None, "grid"))
    out_specs = P("band", "grid", None, None)
    return jax.shard_map(local, mesh=mesh, in_specs=in_specs, out_specs=out_specs, check_vma=False)
```

profile of v0, /device:TPU:0, one launch (start us, length us, event | category | flops | bytes accessed | tf_op | source)
XLA Modules:
  0.0 473.9 jit_solution(9699530073143437805)
XLA Ops:
  0.0 4.3 copy.101
  4.3 7.4 %all-to-all-start = ((bf16[2,32,128,128]{3,1,0,2:T(8,128)(2,1)}), bf16[2,32,128,128]{3,1,0,2:T(8,128)(2,1)S(1)}, u32[]{:S(2)}, u32[]{:S(2)}) async-start(bf16[2,32,128,128]{3,1,0,2:T(8,128)(2,1)} %copy.101), calls=%async_computation | async-start | bytes 4194304 | tf_op jit(solution)/shard_map/all_to_all | solution.py:26
  11.9 48.0 %all-to-all-done = bf16[2,32,128,128]{3,1,0,2:T(8,128)(2,1)S(1)} async-done(((bf16[2,32,128,128]{3,1,0,2:T(8,128)(2,1)}), bf16[2,32,128,128]{3,1,0,2:T(8,128)(2,1)S(1)}, u32[]{:S(2)}, u32[]{:S(2)}) %all-to-all-start) | async-done | bytes 2097184 | tf_op jit(solution)/shard_map/all_to_all | solution.py:26
  59.9 2.7 copy.102
  62.6 2.7 gather_fusion.1
  66.2 2.7 copy.104
  68.9 5.0 %all-to-all-start.1 = ((bf16[2,32,128,128]{3,1,0,2:T(8,128)(2,1)}), bf16[2,32,128,128]{3,1,0,2:T(8,128)(2,1)}, u32[]{:S(2)}, u32[]{:S(2)}) async-start(bf16[2,32,128,128]{3,1,0,2:T(8,128)(2,1)} %copy.104), calls=%async_computation.1 | async-start | bytes 4194304 | tf_op jit(solution)/shard_map/all_to_all | solution.py:30
  74.0 2.2 gather_fusion
  77.9 43.8 %all-to-all-done.1 = bf16[2,32,128,128]{3,1,0,2:T(8,128)(2,1)} async-done(((bf16[2,32,128,128]{3,1,0,2:T(8,128)(2,1)}), bf16[2,32,128,128]{3,1,0,2:T(8,128)(2,1)}, u32[]{:S(2)}, u32[]{:S(2)}) %all-to-all-start.1) | async-done | bytes 2097184 | tf_op jit(solution)/shard_map/all_to_all | solution.py:30
  121.8 4.3 copy.105
  126.0 2.5 gather_fusion.2
  128.6 3.7 convolution_convert_fusion
  132.3 1.0 fusion.19
  133.2 1.0 copy-done
  134.3 1.0 fusion.28
  135.2 9.4 %copy.157 = bf16[2,32,128,128]{1,0,3,2:T(2,128)(2,1)} copy(bf16[2,32,128,128]{3,2,1,0:T(8,128)(2,1)S(1)} %fusion.28) | data formatting | bytes 4194304 | tf_op jit(solution)/shard_map/reshape | solution.py:80
  144.6 10.5 %reshape.144 = bf16[4,2,131072]{2,1,0:T(2,128)(2,1)} reshape(bf16[16384,2,32]{2,1,0:T(2,128)(2,1)} %bitcast.125) | data formatting | bytes 4194304
  155.1 3.8 all-to-all-start.3
  158.9 2.7 fusion.23
  161.7 2.3 fusion.25
  164.0 13.7 %copy.153 = bf16[2,32,128,128]{1,0,3,2:T(2,128)(2,1)} copy(bf16[2,32,128,128]{3,2,1,0:T(8,128)(2,1)} %fusion.25) | data formatting | bytes 4194304 | tf_op jit(solution)/shard_map/reshape | solution.py:79
  177.7 10.6 %reshape.146 = bf16[4,2,131072]{2,1,0:T(2,128)(2,1)} reshape(bf16[16384,2,32]{2,1,0:T(2,128)(2,1)} %bitcast.126) | data formatting | bytes 4194304
  188.3 4.5 all-to-all-start.2
  192.7 1.3 multiply_bitcast_fusion
  194.1 1.3 copy.116
  196.1 7.5 %scatter_custom_fusion = f32[128,4096]{0,1:T(8,128)} fusion(s32[2048]{0:T(1024)S(1)} %compare_select_fusion, f32[2048,128]{1,0:T(8,128)} %copy.116, f32[]{:T(128)} %constant.128.clone.1), kind=kCustom, calls=%fused_computation.58 | custom fusion | bytes 2097664 | tf_op jit(solution)/shard_map/scatter | solution.py:90
  203.6 2.9 copy.117
  206.6 5.6 %reshape.145 = bf16[16384,2,32]{2,1,0:T(2,128)(2,1)} reshape(bf16[4,2,131072]{2,1,0:T(2,128)(2,1)S(1)} %all-to-all-done.3) | data formatting | bytes 4194304
  212.2 16.7 %copy.114 = bf16[2,32,4,4096]{3,1,2,0:T(8,128)(2,1)S(1)} copy(bf16[2,32,4,4096]{1,0,3,2:T(2,128)(2,1)} %bitcast.127) | data formatting | bytes 4194304 | tf_op jit(solution)/shard_map/all_to_all | solution.py:93
  228.9 3.0 fusion.55
  231.9 7.4 %reshape.147 = bf16[16384,2,32]{2,1,0:T(2,128)(2,1)} reshape(bf16[4,2,131072]{2,1,0:T(2,128)(2,1)} %all-to-all-done.2) | data formatting | bytes 4194304
  239.3 18.0 %copy.109 = bf16[2,32,4,4096]{3,1,2,0:T(8,128)(2,1)} copy(bf16[2,32,4,4096]{1,0,3,2:T(2,128)(2,1)} %bitcast.128) | data formatting | bytes 4194304 | tf_op jit(solution)/shard_map/all_to_all | solution.py:92
  257.4 2.7 fusion.57
  260.2 3.2 fusion.8
  263.4 0.9 fusion.59
  264.7 1.0 fusion.9
  265.7 1.3 copy-done.8
  267.1 0.9 fusion.6
  268.0 3.5 copy.123
  271.5 4.6 all-to-all-start.5
  276.1 0.9 fusion.61
  277.7 0.9 fusion.7
  278.6 3.5 copy.120
  282.2 19.6 %all-to-all-done.5 = bf16[2,128,4096]{2,0,1:T(2,128)(2,1)} async-done(((bf16[2,128,4096]{2,0,1:T(2,128)(2,1)}), bf16[2,128,4096]{2,0,1:T(2,128)(2,1)}, u32[]{:S(2)}, u32[]{:S(2)}) %all-to-all-start.5) | async-done | bytes 2097184 | tf_op jit(solution)/shard_map/all_to_all | solution.py:109
  301.8 4.8 %all-to-all-start.4 = ((bf16[2,128,4096]{2,0,1:T(2,128)(2,1)}), bf16[2,128,4096]{2,0,1:T(2,128)(2,1)}, u32[]{:S(2)}, u32[]{:S(2)}) async-start(bf16[2,128,4096]{2,0,1:T(2,128)(2,1)} %copy.120), calls=%async_computation.4 | async-start | bytes 4194304 | tf_op jit(solution)/shard_map/all_to_all | solution.py:108
  308.1 4.8 %copy.163 = bf16[2,4,32,4096]{3,1,2,0:T(4,128)(2,1)} copy(bf16[2,4,32,4096]{3,0,2,1:T(2,128)(2,1)} %bitcast.39) | data formatting | bytes 4194304 | tf_op jit(solution)/shard_map/all_to_all | solution.py:109
  312.9 3.8 reshape.63
  316.7 3.1 fusion.43
  319.8 12.6 %all-to-all-done.4 = bf16[2,128,4096]{2,0,1:T(2,128)(2,1)} async-done(((bf16[2,128,4096]{2,0,1:T(2,128)(2,1)}), bf16[2,128,4096]{2,0,1:T(2,128)(2,1)}, u32[]{:S(2)}, u32[]{:S(2)}) %all-to-all-start.4) | async-done | bytes 2097184 | tf_op jit(solution)/shard_map/all_to_all | solution.py:108
  332.4 4.8 %copy.164 = bf16[2,4,32,4096]{3,1,2,0:T(4,128)(2,1)} copy(bf16[2,4,32,4096]{3,0,2,1:T(2,128)(2,1)} %bitcast.34) | data formatting | bytes 4194304 | tf_op jit(solution)/shard_map/all_to_all | solution.py:108
  337.2 4.8 %reshape.62 = bf16[2,32,128,128]{3,2,1,0:T(8,128)(2,1)} reshape(bf16[2,32,4,4096]{3,2,1,0:T(4,128)(2,1)} %bitcast.138) | data formatting | bytes 4194304 | tf_op jit(solution)/shard_map/reshape | solution.py:110
  342.0 2.9 fusion.45
  345.5 1.1 fusion.32
  346.6 1.2 fusion.31
  348.2 4.8 %select_reduce_fusion.1 = (bf16[32,128,128]{2,1,0:T(8,128)(2,1)S(1)}, bf16[32,128,128]{2,1,0:T(8,128)(2,1)S(1)}, f32[2,32,128,128]{3,2,1,0:T(8,128)}) fusion(bf16[2,32,128,128]{3,2,1,0:T(8,128)(2,1)S(1)} %copy-done.12, f32[2]{0:T(128)S(1)} %compare_select_fusion.5, pred[2]{0:T(512)(128)(4,1)S(1)} %get-tuple-element.11, ...), kind=kOutput, calls=%fused_computation.34 | convolution fusion | flops 551682048 | bytes 12648460 | tf_op jit(solution)/shard_map/pxyk,zk->pxyz/dot_general | solution.py:21
  353.2 1.4 copy.129
  354.6 51.4 %all_to_all.86 = bf16[2,32,128,128]{3,1,0,2:T(8,128)(2,1)S(1)} all-to-all(bf16[2,32,128,128]{3,1,0,2:T(8,128)(2,1)S(1)} %copy.129), channel_id=1, replica_groups=mesh['band'=8,'grid'=4] {'band'}, dimensions={2} | all-to-all | bytes 4194304 | tf_op jit(solution)/shard_map/all_to_all | solution.py:35
  406.0 1.4 copy.130
  407.3 2.3 gather_fusion.5
  409.6 2.2 copy.131
  412.6 2.7 copy.132
  415.2 4.5 all-to-all-start.7
  420.4 46.7 %all-to-all-done.7 = bf16[2,32,128,128]{3,1,0,2:T(8,128)(2,1)} async-done(((bf16[2,32,128,128]{3,1,0,2:T(8,128)(2,1)}), bf16[2,32,128,128]{3,1,0,2:T(8,128)(2,1)}, u32[]{:S(2)}, u32[]{:S(2)}) %all-to-all-start.7) | async-done | bytes 2097184 | tf_op jit(solution)/shard_map/all_to_all | solution.py:41
  467.0 6.7 %fusion.12 = f32[2,32,128,128]{3,2,1,0:T(8,128)} fusion(f32[2,32,128,128]{3,2,1,0:T(8,128)} %get-tuple-element.9, bf16[2,32,128,128]{3,1,0,2:T(8,128)(2,1)} %all-to-all-done.7, f32[2]{0:T(128)S(1)} %broadcast_select_fusion.2, bf16[2,32,128,128]{3,2,1,0:T(8,128)(2,1)S(1)} %copy-done.4, pred[2]{0:T(512)(128)(4,1)S(1)} %compare_and_fusion.1), kind=kLoop, calls=%fused_computation.26 | loop fusion | flops 7340032 | bytes 12582922 | tf_op jit(solution)/shard_map/neg | solution.py:137
  (56 shorter events, 7.6 us)
Async XLA Ops:
  4.3 7.4 %copy-start.15 = (s32[8]{0:T(128)S(1)}, s32[8]{0:T(128)}, u32[]{:S(2)}) copy-start(s32[8]{0:T(128)} %param.11) | copy-start | bytes 100
  4.3 55.7 %all-to-all-start = ((bf16[2,32,128,128]{3,1,0,2:T(8,128)(2,1)}), bf16[2,32,128,128]{3,1,0,2:T(8,128)(2,1)S(1)}, u32[]{:S(2)}, u32[]{:S(2)}) async-start(bf16[2,32,128,128]{3,1,0,2:T(8,128)(2,1)} %copy.101), calls=%async_computation | async-start | bytes 4194304 | tf_op jit(solution)/shard_map/all_to_all | solution.py:26
  68.9 5.0 %copy-start.13 = (bf16[2,32,128,128]{3,2,1,0:T(8,128)(2,1)S(1)}, bf16[2,32,128,128]{3,2,1,0:T(8,128)(2,1)}, u32[]{:S(2)}) copy-start(bf16[2,32,128,128]{3,2,1,0:T(8,128)(2,1)} %param.9) | copy-start | bytes 6291460
  68.9 52.8 %all-to-all-start.1 = ((bf16[2,32,128,128]{3,1,0,2:T(8,128)(2,1)}), bf16[2,32,128,128]{3,1,0,2:T(8,128)(2,1)}, u32[]{:S(2)}, u32[]{:S(2)}) async-start(bf16[2,32,128,128]{3,1,0,2:T(8,128)(2,1)} %copy.104), calls=%async_computation.1 | async-start | bytes 4194304 | tf_op jit(solution)/shard_map/all_to_all | solution.py:30
  128.6 3.7 copy-start.3
  132.2 2.0 copy-start
  155.1 33.1 %all-to-all-start.3 = ((bf16[4,2,131072]{2,1,0:T(2,128)(2,1)}), bf16[4,2,131072]{2,1,0:T(2,128)(2,1)S(1)}, u32[]{:S(2)}, u32[]{:S(2)}) async-start(bf16[4,2,131072]{2,1,0:T(2,128)(2,1)} %reshape.144), calls=%async_computation.3 | async-start | bytes 4194304 | tf_op jit(solution)/shard_map/all_to_all | solution.py:93
  158.9 2.8 copy-start.1
  188.3 43.6 %all-to-all-start.2 = ((bf16[4,2,131072]{2,1,0:T(2,128)(2,1)}), bf16[4,2,131072]{2,1,0:T(2,128)(2,1)}, u32[]{:S(2)}, u32[]{:S(2)}) async-start(bf16[4,2,131072]{2,1,0:T(2,128)(2,1)} %reshape.146), calls=%async_computation.2 | async-start | bytes 4194304 | tf_op jit(solution)/shard_map/all_to_all | solution.py:92
  257.4 2.7 copy-start.2
  257.4 2.9 copy-start.5
  263.4 1.3 copy-start.6
  265.7 1.3 copy-start.8
  271.5 4.6 copy-start.9
  271.5 30.3 %all-to-all-start.5 = ((bf16[2,128,4096]{2,0,1:T(2,128)(2,1)}), bf16[2,128,4096]{2,0,1:T(2,128)(2,1)}, u32[]{:S(2)}, u32[]{:S(2)}) async-start(bf16[2,128,4096]{2,0,1:T(2,128)(2,1)} %copy.123), calls=%async_computation.5 | async-start | bytes 4194304 | tf_op jit(solution)/shard_map/all_to_all | solution.py:109
  276.1 1.6 copy-start.7
  282.2 25.1 %copy-start.14 = (f32[16]{0:T(128)S(1)}, f32[16]{0:T(128)}, u32[]{:S(2)}) copy-start(f32[16]{0:T(128)} %param.10) | copy-start | bytes 196
  301.8 30.6 %all-to-all-start.4 = ((bf16[2,128,4096]{2,0,1:T(2,128)(2,1)}), bf16[2,128,4096]{2,0,1:T(2,128)(2,1)}, u32[]{:S(2)}, u32[]{:S(2)}) async-start(bf16[2,128,4096]{2,0,1:T(2,128)(2,1)} %copy.120), calls=%async_computation.4 | async-start | bytes 4194304 | tf_op jit(solution)/shard_map/all_to_all | solution.py:108
  342.0 2.9 copy-start.10
  342.0 3.5 copy-start.11
  346.6 1.6 copy-start.12
  415.2 51.8 %copy-start.4 = (bf16[2,32,128,128]{3,2,1,0:T(8,128)(2,1)S(1)}, bf16[2,32,128,128]{3,2,1,0:T(8,128)(2,1)}, u32[]{:S(2)}) copy-start(bf16[2,32,128,128]{3,2,1,0:T(8,128)(2,1)} %copy-done.3) | copy-start | bytes 6291460
  415.2 51.8 %all-to-all-start.7 = ((bf16[2,32,128,128]{3,1,0,2:T(8,128)(2,1)}), bf16[2,32,128,128]{3,1,0,2:T(8,128)(2,1)}, u32[]{:S(2)}, u32[]{:S(2)}) async-start(bf16[2,32,128,128]{3,1,0,2:T(8,128)(2,1)} %copy.132), calls=%async_computation.7 | async-start | bytes 4194304 | tf_op jit(solution)/shard_map/all_to_all | solution.py:41
where the time goes:
time: 481 us; the launch traced here: 474 us
  waiting for transfers between devices  171 us (36%)
  local copies, waits for them, and re-layouts  167 us (35%)
  blocking collectives  51.4 us (11%)
  matrix products  37.3 us (8%)
  starting transfers between devices  34.6 us (7%)
  other arithmetic  10.5 us (2%)
    all_to_all x1, blocking collectives, return_block(): lax.all_to_all(block_data.astype(jnp.bfloat16), 'band', split_axis=2, con...  51.4 us
    all_to_all x1, waiting for transfers between devices, fetch_block(): lax.all_to_all(block_data, 'band', split_axis=2, concat_axis=2, tiled=True)  48 us
    all_to_all x1, waiting for transfers between devices, return_block(): lax.all_to_all(pieces.astype(jnp.bfloat16), 'band', split_axis=2, concat_...  46.7 us
    all_to_all x1, waiting for transfers between devices, fetch_block(): lax.all_to_all(pieces, 'band', split_axis=2, concat_axis=2, tiled=True)  43.8 us
    unnamed x37, local copies, waits for them, and re-layouts  43.1 us
    dot_general x18, matrix products, contract(): jnp.einsum(pattern, left_side, right_side, preferred_element_type=jnp.flo...  37.3 us
    all_to_all x1, waiting for transfers between devices, local(): lax.all_to_all(third_imag, 'grid', split_axis=1, concat_axis=2, tiled=True)  19.6 us
    all_to_all x1, local copies, waits for them, and re-layouts, local(): lax.all_to_all(second_real, 'grid', split_axis=2, concat_axis=1, tiled=True)  18 us
  transfers between devices with their start and end apart: 7, of which 5 were waited for; matrix products, arithmetic and copies ran while one was open for 19% of the time, Pallas kernels for 0%

commit v1 on v0

--- a/solution.py
+++ b/solution.py
@@ -23,7 +23,17 @@
 
 def fetch_block(block_data, partner):
     band_count = lax.axis_size("band")
-    spread = lax.all_to_all(block_data, "band", split_axis=2, concat_axis=2, tiled=True)
+    raw_out, a_now = (lax.axis_size("band"), lax.axis_index("band"))
+    r1 = block_data.shape[2] // raw_out
+    r2 = jnp.roll(block_data, -a_now * r1, axis=2)
+    pieces_in = [lax.slice_in_dim(r2, 0, r1, axis=2)]
+    for u in [*range(1, raw_out)]:
+        h_now = lax.slice_in_dim(r2, u * r1, (u + 1) * r1, axis=2)
+        pieces_in.append(
+            lax.ppermute(h_now, "band", [(nth, (nth + u) % raw_out) for nth in range(raw_out)])
+        )
+    aux = jnp.concatenate(pieces_in[::-1], axis=2)
+    spread = jnp.roll(aux, shift=(a_now + 1) * pieces_in[0].shape[2], axis=2)
     dims = spread.shape
     pieces = spread.reshape(dims[0], dims[1], band_count, dims[2] // band_count, dims[3])
     pieces = jnp.take(pieces, partner, axis=2).reshape(dims)

time: 481 us -> 478 us (level)
  waiting for transfers between devices: 171 us -> 161 us
    all_to_all x1 -> x0, waiting for transfers between devices: 48 us -> none  [fetch_block(): lax.all_to_all(block_data, 'band', split_axis=2, concat_axis=2, tiled=True)]
    ppermute x0 -> x7, waiting for transfers between devices: none -> 38.4 us  [fetch_block(): lax.ppermute(h_now, 'band', [(nth, (nth + u) % raw_out) for nth in range(...]
    ppermute x0 -> x7, starting transfers between devices: none -> 9.47 us  [fetch_block(): lax.ppermute(h_now, 'band', [(nth, (nth + u) % raw_out) for nth in range(...]
    all_to_all x1 -> x0, starting transfers between devices: 7.44 us -> none  [fetch_block(): lax.all_to_all(block_data, 'band', split_axis=2, concat_axis=2, tiled=True)]
    unnamed x37 -> x43, local copies, waits for them, and re-layouts: 43.1 us -> 43.9 us
  transfers between devices with their start and end apart: 7 -> 13, of which waited for: 5 -> 8; matrix products, arithmetic and copies ran while one was open for 19% -> 20% of each run, Pallas kernels for 0% -> 0%
where the time goes in v1:
time: 478 us; the launch traced here: 471 us
  local copies, waits for them, and re-layouts  168 us (35%)
  waiting for transfers between devices  161 us (34%)
  blocking collectives  51.4 us (11%)
  matrix products  37.3 us (8%)
  starting transfers between devices  36.6 us (8%)
  other arithmetic  14.1 us (3%)
    all_to_all x1, blocking collectives, return_block(): lax.all_to_all(block_data.astype(jnp.bfloat16), 'band', split_axis=2, con...  51.4 us
    all_to_all x1, waiting for transfers between devices, return_block(): lax.all_to_all(pieces.astype(jnp.bfloat16), 'band', split_axis=2, concat_...  46.7 us
    unnamed x43, local copies, waits for them, and re-layouts  43.9 us
    all_to_all x1, waiting for transfers between devices, fetch_block(): lax.all_to_all(pieces, 'band', split_axis=2, concat_axis=2, tiled=True)  43.7 us
    ppermute x7, waiting for transfers between devices, fetch_block(): lax.ppermute(h_now, 'band', [(nth, (nth + u) % raw_out) for nth in range(...  38.4 us
    dot_general x18, matrix products, contract(): jnp.einsum(pattern, left_side, right_side, preferred_element_type=jnp.flo...  37.3 us
    all_to_all x1, waiting for transfers between devices, local(): lax.all_to_all(third_imag, 'grid', split_axis=1, concat_axis=2, tiled=True)  19.6 us
    all_to_all x1, local copies, waits for them, and re-layouts, local(): lax.all_to_all(second_real, 'grid', split_axis=2, concat_axis=1, tiled=True)  18 us
  transfers between devices with their start and end apart: 13, of which 8 were waited for; matrix products, arithmetic and copies ran while one was open for 20% of the time, Pallas kernels for 0%

profile of v1, /device:TPU:0, one launch (start us, length us, event | category | flops | bytes accessed | tf_op | source)
XLA Modules:
  0.0 470.8 jit_solution(2341656597642316837)
XLA Ops:
  0.0 2.5 fusion.19
  2.5 1.2 fusion.134
  3.7 6.0 %collective-permute-start = (bf16[2,32,16,128]{3,2,1,0:T(8,128)(2,1)}, bf16[2,32,16,128]{3,2,1,0:T(8,128)(2,1)}, u32[]{:S(2)}, u32[]{:S(2)}) collective-permute-start(bf16[2,32,16,128]{3,2,1,0:T(8,128)(2,1)} %get-tuple-element.14), channel_id=1, source_target_pairs={{0,28},{4,0},{8,4},{12,8},{16,12},{20,16},{24,20},{28,24},{1,29},{... | collective-permute-start | bytes 786440 | tf_op jit(solution)/shard_map/ppermute | solution.py:33
  10.2 3.0 collective-permute-start.3
  13.4 3.5 collective-permute-done
  17.8 4.6 collective-permute-done.1
  23.4 4.6 collective-permute-done.2
  29.0 25.8 %collective-permute-done.3 = bf16[2,32,16,128]{3,2,1,0:T(8,128)(2,1)} collective-permute-done((bf16[2,32,16,128]{3,2,1,0:T(8,128)(2,1)S(1)}, bf16[2,32,16,128]{3,2,1,0:T(8,128)(2,1)}, u32[]{:S(2)}, u32[]{:S(2)}) %collective-permute-start.3) | collective-permute-done | bytes 262176 | tf_op jit(solution)/shard_map/ppermute | solution.py:33
  55.8 1.0 constant_dynamic-update-slice_fusion.2
  57.0 1.1 fusion.18
  58.1 2.3 gather_fusion.1
  60.3 2.2 copy.97
  62.9 2.7 copy.98
  65.6 5.0 %all-to-all-start = ((bf16[2,32,128,128]{3,1,0,2:T(8,128)(2,1)}), bf16[2,32,128,128]{3,1,0,2:T(8,128)(2,1)}, u32[]{:S(2)}, u32[]{:S(2)}) async-start(bf16[2,32,128,128]{3,1,0,2:T(8,128)(2,1)} %copy.98), calls=%async_computation | async-start | bytes 4194304 | tf_op jit(solution)/shard_map/all_to_all | solution.py:40
  71.8 2.2 gather_fusion
  74.6 43.7 %all-to-all-done = bf16[2,32,128,128]{3,1,0,2:T(8,128)(2,1)} async-done(((bf16[2,32,128,128]{3,1,0,2:T(8,128)(2,1)}), bf16[2,32,128,128]{3,1,0,2:T(8,128)(2,1)}, u32[]{:S(2)}, u32[]{:S(2)}) %all-to-all-start) | async-done | bytes 2097184 | tf_op jit(solution)/shard_map/all_to_all | solution.py:40
  118.3 4.3 copy.99
  122.5 2.5 gather_fusion.2
  125.1 3.7 convolution_convert_fusion
  129.7 1.0 copy-done
  131.7 9.4 %copy.151 = bf16[2,32,128,128]{1,0,3,2:T(2,128)(2,1)} copy(bf16[2,32,128,128]{3,2,1,0:T(8,128)(2,1)S(1)} %fusion.30) | data formatting | bytes 4194304 | tf_op jit(solution)/shard_map/reshape | solution.py:90
  141.2 10.5 %reshape.144 = bf16[4,2,131072]{2,1,0:T(2,128)(2,1)} reshape(bf16[16384,2,32]{2,1,0:T(2,128)(2,1)} %bitcast.125) | data formatting | bytes 4194304
  151.7 3.8 all-to-all-start.2
  155.5 2.7 fusion.25
  158.3 2.3 fusion.27
  160.6 13.8 %copy.147 = bf16[2,32,128,128]{1,0,3,2:T(2,128)(2,1)} copy(bf16[2,32,128,128]{3,2,1,0:T(8,128)(2,1)} %fusion.27) | data formatting | bytes 4194304 | tf_op jit(solution)/shard_map/reshape | solution.py:89
  174.4 10.6 %reshape.146 = bf16[4,2,131072]{2,1,0:T(2,128)(2,1)} reshape(bf16[16384,2,32]{2,1,0:T(2,128)(2,1)} %bitcast.126) | data formatting | bytes 4194304
  185.0 4.5 all-to-all-start.1
  189.4 1.3 multiply_bitcast_fusion
  190.7 1.3 copy.110
  192.8 7.5 %scatter_custom_fusion = f32[128,4096]{0,1:T(8,128)} fusion(s32[2048]{0:T(1024)S(1)} %compare_select_fusion, f32[2048,128]{1,0:T(8,128)} %copy.110, f32[]{:T(128)} %constant.147.clone.1), kind=kCustom, calls=%fused_computation.64 | custom fusion | bytes 2097664 | tf_op jit(solution)/shard_map/scatter | solution.py:100
  200.3 2.9 copy.111
  203.3 5.6 %reshape.145 = bf16[16384,2,32]{2,1,0:T(2,128)(2,1)} reshape(bf16[4,2,131072]{2,1,0:T(2,128)(2,1)S(1)} %all-to-all-done.2) | data formatting | bytes 4194304
  208.9 16.7 %copy.108 = bf16[2,32,4,4096]{3,1,2,0:T(8,128)(2,1)S(1)} copy(bf16[2,32,4,4096]{1,0,3,2:T(2,128)(2,1)} %bitcast.127) | data formatting | bytes 4194304 | tf_op jit(solution)/shard_map/all_to_all | solution.py:103
  225.6 3.0 fusion.57
  228.6 7.4 %reshape.147 = bf16[16384,2,32]{2,1,0:T(2,128)(2,1)} reshape(bf16[4,2,131072]{2,1,0:T(2,128)(2,1)} %all-to-all-done.1) | data formatting | bytes 4194304
  236.1 18.0 %copy.103 = bf16[2,32,4,4096]{3,1,2,0:T(8,128)(2,1)} copy(bf16[2,32,4,4096]{1,0,3,2:T(2,128)(2,1)} %bitcast.128) | data formatting | bytes 4194304 | tf_op jit(solution)/shard_map/all_to_all | solution.py:102
  254.1 2.7 fusion.59
  256.9 3.2 fusion.8
  262.4 1.4 copy-done.8
  264.7 3.5 copy.117
  268.3 4.6 all-to-all-start.4
  275.4 3.6 copy.114
  279.0 19.6 %all-to-all-done.4 = bf16[2,128,4096]{2,0,1:T(2,128)(2,1)} async-done(((bf16[2,128,4096]{2,0,1:T(2,128)(2,1)}), bf16[2,128,4096]{2,0,1:T(2,128)(2,1)}, u32[]{:S(2)}, u32[]{:S(2)}) %all-to-all-start.4) | async-done | bytes 2097184 | tf_op jit(solution)/shard_map/all_to_all | solution.py:119
  298.6 4.9 %all-to-all-start.3 = ((bf16[2,128,4096]{2,0,1:T(2,128)(2,1)}), bf16[2,128,4096]{2,0,1:T(2,128)(2,1)}, u32[]{:S(2)}, u32[]{:S(2)}) async-start(bf16[2,128,4096]{2,0,1:T(2,128)(2,1)} %copy.114), calls=%async_computation.3 | async-start | bytes 4194304 | tf_op jit(solution)/shard_map/all_to_all | solution.py:118
  304.8 4.8 %copy.157 = bf16[2,4,32,4096]{3,1,2,0:T(4,128)(2,1)} copy(bf16[2,4,32,4096]{3,0,2,1:T(2,128)(2,1)} %bitcast.39) | data formatting | bytes 4194304 | tf_op jit(solution)/shard_map/all_to_all | solution.py:119
  309.7 3.8 reshape.63
  313.4 3.1 fusion.45
  316.6 12.6 %all-to-all-done.3 = bf16[2,128,4096]{2,0,1:T(2,128)(2,1)} async-done(((bf16[2,128,4096]{2,0,1:T(2,128)(2,1)}), bf16[2,128,4096]{2,0,1:T(2,128)(2,1)}, u32[]{:S(2)}, u32[]{:S(2)}) %all-to-all-start.3) | async-done | bytes 2097184 | tf_op jit(solution)/shard_map/all_to_all | solution.py:118
  329.2 4.9 %copy.158 = bf16[2,4,32,4096]{3,1,2,0:T(4,128)(2,1)} copy(bf16[2,4,32,4096]{3,0,2,1:T(2,128)(2,1)} %bitcast.34) | data formatting | bytes 4194304 | tf_op jit(solution)/shard_map/all_to_all | solution.py:118
  334.0 4.8 %reshape.62 = bf16[2,32,128,128]{3,2,1,0:T(8,128)(2,1)} reshape(bf16[2,32,4,4096]{3,2,1,0:T(4,128)(2,1)} %bitcast.138) | data formatting | bytes 4194304 | tf_op jit(solution)/shard_map/reshape | solution.py:120
  338.8 2.9 fusion.47
  342.3 1.1 fusion.34
  343.4 1.2 fusion.33
  345.0 4.8 %select_reduce_fusion.1 = (bf16[32,128,128]{2,1,0:T(8,128)(2,1)S(1)}, bf16[32,128,128]{2,1,0:T(8,128)(2,1)S(1)}, f32[2,32,128,128]{3,2,1,0:T(8,128)}) fusion(bf16[2,32,128,128]{3,2,1,0:T(8,128)(2,1)S(1)} %copy-done.12, f32[2]{0:T(128)S(1)} %compare_select_fusion.5, pred[2]{0:T(512)(128)(4,1)S(1)} %get-tuple-element.19, ...), kind=kOutput, calls=%fused_computation.38 | convolution fusion | flops 551682048 | bytes 12648460 | tf_op jit(solution)/shard_map/pxyk,zk->pxyz/dot_general | solution.py:21
  350.0 1.4 copy.123
  351.4 51.4 %all_to_all.81 = bf16[2,32,128,128]{3,1,0,2:T(8,128)(2,1)S(1)} all-to-all(bf16[2,32,128,128]{3,1,0,2:T(8,128)(2,1)S(1)} %copy.123), channel_id=1, replica_groups=mesh['band'=8,'grid'=4] {'band'}, dimensions={2} | all-to-all | bytes 4194304 | tf_op jit(solution)/shard_map/all_to_all | solution.py:45
  402.8 1.4 copy.124
  404.2 2.3 gather_fusion.5
  406.5 2.2 copy.125
  409.4 2.7 copy.126
  412.1 4.5 all-to-all-start.6
  417.2 46.7 %all-to-all-done.6 = bf16[2,32,128,128]{3,1,0,2:T(8,128)(2,1)} async-done(((bf16[2,32,128,128]{3,1,0,2:T(8,128)(2,1)}), bf16[2,32,128,128]{3,1,0,2:T(8,128)(2,1)}, u32[]{:S(2)}, u32[]{:S(2)}) %all-to-all-start.6) | async-done | bytes 2097184 | tf_op jit(solution)/shard_map/all_to_all | solution.py:51
  463.9 6.7 %fusion.12 = f32[2,32,128,128]{3,2,1,0:T(8,128)} fusion(f32[2,32,128,128]{3,2,1,0:T(8,128)} %get-tuple-element.17, bf16[2,32,128,128]{3,1,0,2:T(8,128)(2,1)} %all-to-all-done.6, f32[2]{0:T(128)S(1)} %broadcast_select_fusion.2, bf16[2,32,128,128]{3,2,1,0:T(8,128)(2,1)S(1)} %copy-done.4, pred[2]{0:T(512)(128)(4,1)S(1)} %compare_and_fusion.1), kind=kLoop, calls=%fused_computation.26 | loop fusion | flops 7340032 | bytes 12582922 | tf_op jit(solution)/shard_map/neg | solution.py:147
  (76 shorter events, 18.1 us)
Async XLA Ops:
  2.5 10.7 %copy-start.15 = (s32[8]{0:T(128)S(1)}, s32[8]{0:T(128)}, u32[]{:S(2)}) copy-start(s32[8]{0:T(128)} %param.13) | copy-start | bytes 100
  3.7 13.1 %collective-permute-start = (bf16[2,32,16,128]{3,2,1,0:T(8,128)(2,1)}, bf16[2,32,16,128]{3,2,1,0:T(8,128)(2,1)}, u32[]{:S(2)}, u32[]{:S(2)}) collective-permute-start(bf16[2,32,16,128]{3,2,1,0:T(8,128)(2,1)} %get-tuple-element.14), channel_id=1, source_target_pairs={{0,28},{4,0},{8,4},{12,8},{16,12},{20,16},{24,20},{28,24},{1,29},{... | collective-permute-start | bytes 786440 | tf_op jit(solution)/shard_map/ppermute | solution.py:33
  9.7 12.7 %collective-permute-start.1 = (bf16[2,32,16,128]{3,2,1,0:T(8,128)(2,1)}, bf16[2,32,16,128]{3,2,1,0:T(8,128)(2,1)}, u32[]{:S(2)}, u32[]{:S(2)}) collective-permute-start(bf16[2,32,16,128]{3,2,1,0:T(8,128)(2,1)} %get-tuple-element.13), channel_id=1, source_target_pairs={{0,24},{4,28},{8,0},{12,4},{16,8},{20,12},{24,16},{28,20},{1,25},{... | collective-permute-start | bytes 786440 | tf_op jit(solution)/shard_map/ppermute | solution.py:33
  10.2 17.9 %collective-permute-start.2 = (bf16[2,32,16,128]{3,2,1,0:T(8,128)(2,1)S(1)}, bf16[2,32,16,128]{3,2,1,0:T(8,128)(2,1)}, u32[]{:S(2)}, u32[]{:S(2)}) collective-permute-start(bf16[2,32,16,128]{3,2,1,0:T(8,128)(2,1)S(1)} %get-tuple-element.12), channel_id=1, source_target_pairs={{0,20},{4,24},{8,28},{12,0},{16,4},{20,8},{24,12},{28,16},{1,21},{... | collective-permute-start | bytes 786440 | tf_op jit(solution)/shard_map/ppermute | solution.py:33
  10.2 44.6 %collective-permute-start.3 = (bf16[2,32,16,128]{3,2,1,0:T(8,128)(2,1)S(1)}, bf16[2,32,16,128]{3,2,1,0:T(8,128)(2,1)}, u32[]{:S(2)}, u32[]{:S(2)}) collective-permute-start(bf16[2,32,16,128]{3,2,1,0:T(8,128)(2,1)S(1)} %get-tuple-element.11), channel_id=1, source_target_pairs={{0,16},{4,20},{8,24},{12,28},{16,0},{20,4},{24,8},{28,12},{1,17},{... | collective-permute-start | bytes 786440 | tf_op jit(solution)/shard_map/ppermute | solution.py:33
  13.2 42.6 %collective-permute-start.4 = (bf16[2,32,16,128]{3,2,1,0:T(8,128)(2,1)S(1)}, bf16[2,32,16,128]{3,2,1,0:T(8,128)(2,1)}, u32[]{:S(2)}, u32[]{:S(2)}) collective-permute-start(bf16[2,32,16,128]{3,2,1,0:T(8,128)(2,1)S(1)} %get-tuple-element.10), channel_id=1, source_target_pairs={{0,12},{4,16},{8,20},{12,24},{16,28},{20,0},{24,4},{28,8},{1,13},{... | collective-permute-start | bytes 786440 | tf_op jit(solution)/shard_map/ppermute | solution.py:33
  16.8 39.9 %collective-permute-start.5 = (bf16[2,32,16,128]{3,2,1,0:T(8,128)(2,1)S(1)}, bf16[2,32,16,128]{3,2,1,0:T(8,128)(2,1)S(1)}, u32[]{:S(2)}, u32[]{:S(2)}) collective-permute-start(bf16[2,32,16,128]{3,2,1,0:T(8,128)(2,1)S(1)} %get-tuple-element.9), channel_id=1, source_target_pairs={{0,8},{4,12},{8,16},{12,20},{16,24},{20,28},{24,0},{28,4},{1,9},{5... | collective-permute-start | bytes 786440 | tf_op jit(solution)/shard_map/ppermute | solution.py:33
  22.4 34.4 %collective-permute-start.6 = (bf16[2,32,16,128]{3,2,1,0:T(8,128)(2,1)S(1)}, bf16[2,32,16,128]{3,2,1,0:T(8,128)(2,1)S(1)}, u32[]{:S(2)}, u32[]{:S(2)}) collective-permute-start(bf16[2,32,16,128]{3,2,1,0:T(8,128)(2,1)S(1)} %get-tuple-element.8), channel_id=1, source_target_pairs={{0,4},{4,8},{8,12},{12,16},{16,20},{20,24},{24,28},{28,0},{1,5},{5... | collective-permute-start | bytes 786440 | tf_op jit(solution)/shard_map/ppermute | solution.py:33
  65.6 6.3 %copy-start.13 = (bf16[2,32,128,128]{3,2,1,0:T(8,128)(2,1)S(1)}, bf16[2,32,128,128]{3,2,1,0:T(8,128)(2,1)}, u32[]{:S(2)}) copy-start(bf16[2,32,128,128]{3,2,1,0:T(8,128)(2,1)} %param.11) | copy-start | bytes 6291460
  65.6 52.7 %all-to-all-start = ((bf16[2,32,128,128]{3,1,0,2:T(8,128)(2,1)}), bf16[2,32,128,128]{3,1,0,2:T(8,128)(2,1)}, u32[]{:S(2)}, u32[]{:S(2)}) async-start(bf16[2,32,128,128]{3,1,0,2:T(8,128)(2,1)} %copy.98), calls=%async_computation | async-start | bytes 4194304 | tf_op jit(solution)/shard_map/all_to_all | solution.py:40
  125.1 3.7 copy-start.3
  128.7 2.0 copy-start
  151.7 33.2 %all-to-all-start.2 = ((bf16[4,2,131072]{2,1,0:T(2,128)(2,1)}), bf16[4,2,131072]{2,1,0:T(2,128)(2,1)S(1)}, u32[]{:S(2)}, u32[]{:S(2)}) async-start(bf16[4,2,131072]{2,1,0:T(2,128)(2,1)} %reshape.144), calls=%async_computation.2 | async-start | bytes 4194304 | tf_op jit(solution)/shard_map/all_to_all | solution.py:103
  155.5 2.8 copy-start.1
  185.0 43.7 %all-to-all-start.1 = ((bf16[4,2,131072]{2,1,0:T(2,128)(2,1)}), bf16[4,2,131072]{2,1,0:T(2,128)(2,1)}, u32[]{:S(2)}, u32[]{:S(2)}) async-start(bf16[4,2,131072]{2,1,0:T(2,128)(2,1)} %reshape.146), calls=%async_computation.1 | async-start | bytes 4194304 | tf_op jit(solution)/shard_map/all_to_all | solution.py:102
  254.1 2.7 copy-start.2
  254.1 2.9 copy-start.5
  260.1 1.3 copy-start.6
  262.4 1.4 copy-start.8
  268.3 4.6 copy-start.9
  268.3 30.3 %all-to-all-start.4 = ((bf16[2,128,4096]{2,0,1:T(2,128)(2,1)}), bf16[2,128,4096]{2,0,1:T(2,128)(2,1)}, u32[]{:S(2)}, u32[]{:S(2)}) async-start(bf16[2,128,4096]{2,0,1:T(2,128)(2,1)} %copy.117), calls=%async_computation.4 | async-start | bytes 4194304 | tf_op jit(solution)/shard_map/all_to_all | solution.py:119
  272.9 1.6 copy-start.7
  278.9 25.1 %copy-start.14 = (f32[16]{0:T(128)S(1)}, f32[16]{0:T(128)}, u32[]{:S(2)}) copy-start(f32[16]{0:T(128)} %param.12) | copy-start | bytes 196
  298.6 30.6 %all-to-all-start.3 = ((bf16[2,128,4096]{2,0,1:T(2,128)(2,1)}), bf16[2,128,4096]{2,0,1:T(2,128)(2,1)}, u32[]{:S(2)}, u32[]{:S(2)}) async-start(bf16[2,128,4096]{2,0,1:T(2,128)(2,1)} %copy.114), calls=%async_computation.3 | async-start | bytes 4194304 | tf_op jit(solution)/shard_map/all_to_all | solution.py:118
  338.8 2.9 copy-start.10
  338.8 3.5 copy-start.11
  343.4 1.6 copy-start.12
  412.1 51.8 %copy-start.4 = (bf16[2,32,128,128]{3,2,1,0:T(8,128)(2,1)S(1)}, bf16[2,32,128,128]{3,2,1,0:T(8,128)(2,1)}, u32[]{:S(2)}) copy-start(bf16[2,32,128,128]{3,2,1,0:T(8,128)(2,1)} %copy-done.3) | copy-start | bytes 6291460
  412.1 51.8 %all-to-all-start.6 = ((bf16[2,32,128,128]{3,1,0,2:T(8,128)(2,1)}), bf16[2,32,128,128]{3,1,0,2:T(8,128)(2,1)}, u32[]{:S(2)}, u32[]{:S(2)}) async-start(bf16[2,32,128,128]{3,1,0,2:T(8,128)(2,1)} %copy.126), calls=%async_computation.6 | async-start | bytes 4194304 | tf_op jit(solution)/shard_map/all_to_all | solution.py:51
